TPU v7x, 512 devices: a whole 4x8x8 slice. The times are simulated.
512 devices in a mesh: seq: 128 (over z_hi, y, x, core), chan: 4 (over z_lo).
Axes of the slice: x: 4, y: 8, z: 8 (z_hi: 2, z_lo: 4; z = z_hi * 4 + z_lo), core: 2. Of those that a mesh axis runs over, the one named last changes fastest.
Arguments:
- latent: bfloat16 [65536, 16], P(('seq', 'chan')), may hold values from -140 to 140
- in_weight: bfloat16 [9, 16, 384], P(None, 'chan'), may hold values from -2 to 2
- in_bias: float32 [384], P('chan'), may hold values from -1.75 to 1.75
- norm_gain: float32 [3, 2, 384], P(None, None, 'chan'), may hold values from 0.1 to 1.9
- norm_shift: float32 [3, 2, 384], P(None, None, 'chan'), may hold values from -1.75 to 1.75
- res_weight: bfloat16 [3, 2, 9, 384, 384], P(None, None, None, 'chan'), may hold values from -2 to 2
- res_bias: float32 [3, 2, 384], P(None, None, 'chan'), may hold values from -1.75 to 1.75
- up_weight: bfloat16 [9, 384, 192], P(None, 'chan'), may hold values from -0.109375 to 0.109375
- up_bias: float32 [192], P('chan'), may hold values from -1.75 to 1.75
Outputs:
- image: bfloat16 [192, 512, 512], P('chan', 'seq')
All inputs are finite; a program needn't handle non-finite values.
Results may differ from a plain program's by a relative error of at most 0.022.
Values may be sent and summed in bfloat16 or wider, within the bound.
A program may use at most 64 MiB of HBM per device.

v0:
```python
import jax
import jax.numpy as jnp
from jax import lax
from jax.sharding import PartitionSpec as P

CH = 384
LAYERS = 3
LAT_W = 256


EPS = 1e-06


def padded_2(array, sides, width):
    for axis, dim in sides:
        peers, length = (lax.axis_size(axis), array.shape[dim])
        up = [(i, (i + 1) % peers) for i in range(peers - 1)]
        down = [(j, i) for i, j in up]
        last = lax.slice_in_dim(array, length - width, length, axis=dim)
        first = lax.slice_in_dim(array, 0, width, axis=dim)
        before = lax.ppermute(last, axis, up)
        after = lax.ppermute(first, axis, down)
        array = jnp.concatenate([before, array, after], axis=dim)
    return array


def with_rims(field):
    return padded_2(field, (("seq", 1),), 1)


def gather_columns(padded):
    chans = padded.shape[0]
    height = padded.shape[1] - 2
    width = padded.shape[2]
    framed = jnp.pad(padded, ((0, 0), (0, 0), (1, 1)))
    shifted = [
        framed[:, row_off : row_off + height, col_off : col_off + width]
        for row_off in range(3)
        for col_off in range(3)
    ]
    return jnp.stack(shifted, 0).reshape(9 * chans, height * width)


def contract(flat_weight, columns):
    return lax.dot_general(
        flat_weight, columns, (((0,), (0,)), ((), ())), preferred_element_type=jnp.float32
    )


def conv_block(padded, weight, bias):
    columns = gather_columns(padded)
    flat_weight = weight.reshape(-1, weight.shape[2])
    out_share = flat_weight.shape[1] // lax.axis_size("chan")
    totals = lax.psum(contract(flat_weight, columns).astype(jnp.bfloat16), "chan").astype(
        jnp.float32
    )
    partial_value = lax.dynamic_slice_in_dim(
        totals, lax.axis_index("chan") * out_share, out_share, 0
    )
    return (partial_value + bias[:, None]).reshape(out_share, padded.shape[1] - 2, padded.shape[2])


def up_block(padded, weight, bias):
    columns = gather_columns(padded)
    flat_weight = weight.reshape(-1, weight.shape[2])
    out_share = flat_weight.shape[1] // lax.axis_size("chan")
    totals = lax.psum(contract(flat_weight, columns).astype(jnp.bfloat16), "chan").astype(
        jnp.float32
    )
    partial_value = lax.dynamic_slice_in_dim(
        totals, lax.axis_index("chan") * out_share, out_share, 0
    )
    return (partial_value + bias[:, None]).reshape(out_share, padded.shape[1] - 2, padded.shape[2])


def rms_norm(values, gain_vec, shift_vec):
    squares = jnp.sum(values * values, axis=0)
    totals = lax.psum(squares, "chan")
    scale = lax.rsqrt(totals / float(CH) + EPS)
    return values * scale[None] * gain_vec[:, None, None] + shift_vec[:, None, None]


def body(
    latent, in_weight, in_bias, norm_gain, norm_shift, res_weight, res_bias, up_weight, up_bias
):
    own_quarter = lax.all_to_all(latent, "chan", split_axis=1, concat_axis=0, tiled=True)
    slab_rows = own_quarter.shape[0] // LAT_W
    slab_field = own_quarter.T.reshape(own_quarter.shape[1], slab_rows, LAT_W)
    stream = conv_block(with_rims(slab_field), in_weight, in_bias).astype(jnp.bfloat16)
    for layer_idx in range(LAYERS):
        normed = jax.nn.silu(
            rms_norm(stream.astype(jnp.float32), norm_gain[layer_idx, 0], norm_shift[layer_idx, 0])
        ).astype(jnp.bfloat16)
        middle = conv_block(with_rims(normed), res_weight[layer_idx, 0], res_bias[layer_idx, 0])
        branch_in = jax.nn.silu(
            rms_norm(middle, norm_gain[layer_idx, 1], norm_shift[layer_idx, 1])
        ).astype(jnp.bfloat16)
        branch_out = conv_block(
            with_rims(branch_in), res_weight[layer_idx, 1], res_bias[layer_idx, 1]
        )
        stream = (stream.astype(jnp.float32) + branch_out).astype(jnp.bfloat16)
    rimmed = with_rims(stream)
    widened = jnp.repeat(jnp.repeat(rimmed, 2, axis=1), 2, axis=2)[:, 1:-1, :]
    return up_block(widened, up_weight, up_bias).astype(jnp.bfloat16)


def solution(mesh):
    placed = (
        P(("seq", "chan"), None),
        P(None, "chan", None),
        P("chan"),
        P(None, None, "chan"),
        P(None, None, "chan"),
        P(None, None, None, "chan", None),
        P(None, None, "chan"),
        P(None, "chan", None),
        P("chan"),
    )
    return jax.shard_map(
        body, mesh=mesh, in_specs=placed, out_specs=P("chan", "seq", None), check_vma=False
    )
```

profile of v0, /device:TPU:1, one launch (start us, length us, event | category | flops | bytes accessed | tf_op | source)
XLA Modules:
  0.0 712.8 jit_solution(14718916674875292210)
XLA Ops:
  6.5 12.4 %all_to_all.19 = bf16[128,4,4]{0,2,1:T(4,128)(2,1)S(1)} all-to-all(bf16[128,4,4]{0,2,1:T(4,128)(2,1)} %bitcast.413), channel_id=1, replica_groups=mesh['seq'=128,'chan'=4] {'chan'}, dimensions={1} | all-to-all | bytes 8192 | tf_op jit(solution)/shard_map/all_to_all | solution.py:86
  18.9 5.1 collective-permute-start
  32.1 58.4 %all-reduce.17.cloned.1.call-done = bf16[384,512]{0,1:T(8,128)(2,1)} async-done(((bf16[384,512]{0,1:T(8,128)(2,1)}), bf16[384,512]{0,1:T(8,128)(2,1)}) %all-reduce.17.cloned.1.call-update) | async-done | bytes 393232 | tf_op jit(solution)/shard_map/psum | solution.py:54
  91.6 8.2 %psum.99 = f32[2,256]{1,0:T(2,128)S(1)} all-reduce(f32[2,256]{1,0:T(2,128)S(1)} %reduce_sum.67), channel_id=1, replica_groups=mesh['seq'=128,'chan'=4] {'chan'}, use_global_device_ids=true, to_apply=%region_2.3 | all-reduce | flops 512 | bytes 4096 | tf_op jit(solution)/shard_map/psum | solution.py:78
  100.2 7.0 collective-permute-start.2
  116.9 57.9 %all-reduce.19.cloned.1.call-done = bf16[384,512]{0,1:T(8,128)(2,1)} async-done(((bf16[384,512]{0,1:T(8,128)(2,1)}), bf16[384,512]{0,1:T(8,128)(2,1)}) %all-reduce.19.cloned.1.call-update) | async-done | bytes 393232 | tf_op jit(solution)/shard_map/psum | solution.py:54
  176.0 8.2 %psum.101 = f32[2,256]{1,0:T(2,128)S(1)} all-reduce(f32[2,256]{1,0:T(2,128)S(1)} %reduce_sum.69), channel_id=1, replica_groups=mesh['seq'=128,'chan'=4] {'chan'}, use_global_device_ids=true, to_apply=%region_5.6 | all-reduce | flops 512 | bytes 4096 | tf_op jit(solution)/shard_map/psum | solution.py:78
  185.1 6.9 collective-permute-start.4
  201.6 59.0 %all-reduce.21.cloned.1.call-done = bf16[384,512]{0,1:T(8,128)(2,1)} async-done(((bf16[384,512]{0,1:T(8,128)(2,1)}), bf16[384,512]{0,1:T(8,128)(2,1)}) %all-reduce.21.cloned.1.call-update) | async-done | bytes 393232 | tf_op jit(solution)/shard_map/psum | solution.py:54
  261.8 8.2 %psum.103 = f32[2,256]{1,0:T(2,128)S(1)} all-reduce(f32[2,256]{1,0:T(2,128)S(1)} %reduce_sum.71), channel_id=1, replica_groups=mesh['seq'=128,'chan'=4] {'chan'}, use_global_device_ids=true, to_apply=%region_8.9 | all-reduce | flops 512 | bytes 4096 | tf_op jit(solution)/shard_map/psum | solution.py:78
  270.4 7.0 collective-permute-start.6
  286.2 59.0 %all-reduce.23.cloned.1.call-done = bf16[384,512]{0,1:T(8,128)(2,1)} async-done(((bf16[384,512]{0,1:T(8,128)(2,1)}), bf16[384,512]{0,1:T(8,128)(2,1)}) %all-reduce.23.cloned.1.call-update) | async-done | bytes 393232 | tf_op jit(solution)/shard_map/psum | solution.py:54
  346.3 8.2 %psum.105 = f32[2,256]{1,0:T(2,128)S(1)} all-reduce(f32[2,256]{1,0:T(2,128)S(1)} %reduce_sum.73), channel_id=1, replica_groups=mesh['seq'=128,'chan'=4] {'chan'}, use_global_device_ids=true, to_apply=%region_11.12 | all-reduce | flops 512 | bytes 4096 | tf_op jit(solution)/shard_map/psum | solution.py:78
  354.9 7.0 collective-permute-start.8
  370.6 58.9 %all-reduce.25.cloned.1.call-done = bf16[384,512]{0,1:T(8,128)(2,1)} async-done(((bf16[384,512]{0,1:T(8,128)(2,1)}), bf16[384,512]{0,1:T(8,128)(2,1)}) %all-reduce.25.cloned.1.call-update) | async-done | bytes 393232 | tf_op jit(solution)/shard_map/psum | solution.py:54
  430.9 8.2 %psum.107 = f32[2,256]{1,0:T(2,128)S(1)} all-reduce(f32[2,256]{1,0:T(2,128)S(1)} %reduce_sum.75), channel_id=1, replica_groups=mesh['seq'=128,'chan'=4] {'chan'}, use_global_device_ids=true, to_apply=%region_14.15 | all-reduce | flops 512 | bytes 4096 | tf_op jit(solution)/shard_map/psum | solution.py:78
  439.4 7.0 collective-permute-start.10
  455.1 58.9 %all-reduce.27.cloned.1.call-done = bf16[384,512]{0,1:T(8,128)(2,1)} async-done(((bf16[384,512]{0,1:T(8,128)(2,1)}), bf16[384,512]{0,1:T(8,128)(2,1)}) %all-reduce.27.cloned.1.call-update) | async-done | bytes 393232 | tf_op jit(solution)/shard_map/psum | solution.py:54
  515.2 8.2 %psum.109 = f32[2,256]{1,0:T(2,128)S(1)} all-reduce(f32[2,256]{1,0:T(2,128)S(1)} %reduce_sum.77), channel_id=1, replica_groups=mesh['seq'=128,'chan'=4] {'chan'}, use_global_device_ids=true, to_apply=%region_17.18 | all-reduce | flops 512 | bytes 4096 | tf_op jit(solution)/shard_map/psum | solution.py:78
  523.7 7.0 collective-permute-start.12
  539.5 58.9 %all-reduce.29.cloned.1.call-done = bf16[384,512]{0,1:T(8,128)(2,1)} async-done(((bf16[384,512]{0,1:T(8,128)(2,1)}), bf16[384,512]{0,1:T(8,128)(2,1)}) %all-reduce.29.cloned.1.call-update) | async-done | bytes 393232 | tf_op jit(solution)/shard_map/psum | solution.py:54
  599.6 5.9 collective-permute-start.14
  622.1 10.0 %copy.87 = bf16[9,96,4,512]{3,2,1,0:T(4,128)(2,1)} copy(bf16[9,96,4,512]{1,2,3,0:T(4,128)(2,1)} %bitcast_dynamic-update-slice_fusion) | data formatting | bytes 7077888 | tf_op jit(solution)/shard_map/stack | solution.py:41
  637.3 66.8 %all-reduce.31.cloned.1.call-done = bf16[192,2048]{1,0:T(8,128)(2,1)} async-done(((bf16[192,2048]{1,0:T(8,128)(2,1)}), bf16[192,2048]{1,0:T(8,128)(2,1)}) %all-reduce.31.cloned.1.call-update) | async-done | bytes 786448 | tf_op jit(solution)/shard_map/psum | solution.py:67
  (240 shorter events, 96.0 us)
Async XLA Ops:
  6.5 83.9 %all-reduce.17.cloned.1.call-start = ((), (), s32[]{:S(2)}) async-start(), calls=%async_computation.1 | async-start | bytes 786432 | tf_op jit(solution)/shard_map/psum | solution.py:54
  18.9 7.8 %collective-permute-start = (bf16[4,1,256]{2,1,0:T(2,128)(2,1)S(1)}, bf16[4,1,256]{2,1,0:T(2,128)(2,1)S(1)}, u32[]{:S(2)}, u32[]{:S(2)}) collective-permute-start(bf16[4,1,256]{2,1,0:T(2,128)(2,1)S(1)} %get-tuple-element.41), channel_id=1, source_target_pairs={{0,4},{4,8},{8,12},{12,16},{16,20},{20,24},{24,28},{28,32},{32,36}... | collective-permute-start | bytes 6152 | tf_op jit(solution)/shard_map/ppermute | solution.py:21
  24.0 4.9 collective-permute-start.1
  30.6 144.2 %all-reduce.19.cloned.1.call-start = ((), (), s32[]{:S(2)}) async-start(), calls=%async_computation.2 | async-start | bytes 786432 | tf_op jit(solution)/shard_map/psum | solution.py:54
  100.2 12.7 %collective-permute-start.2 = (bf16[96,1,256]{2,0,1:T(8,128)(2,1)S(1)}, bf16[96,1,256]{2,0,1:T(8,128)(2,1)S(1)}, u32[]{:S(2)}, u32[]{:S(2)}) collective-permute-start(bf16[96,1,256]{2,0,1:T(8,128)(2,1)S(1)} %get-tuple-element.39), channel_id=1, source_target_pairs={{0,4},{4,8},{8,12},{12,16},{16,20},{20,24},{24,28},{28,32},{32,36}... | collective-permute-start | bytes 147464 | tf_op jit(solution)/shard_map/ppermute | solution.py:21
  107.1 5.7 collective-permute-start.3
  116.2 144.3 %all-reduce.21.cloned.1.call-start = ((), (), s32[]{:S(2)}) async-start(), calls=%async_computation.3 | async-start | bytes 786432 | tf_op jit(solution)/shard_map/psum | solution.py:54
  185.1 9.0 %collective-permute-start.4 = (bf16[96,1,256]{2,0,1:T(8,128)(2,1)}, bf16[96,1,256]{2,0,1:T(8,128)(2,1)S(1)}, u32[]{:S(2)}, u32[]{:S(2)}) collective-permute-start(bf16[96,1,256]{2,0,1:T(8,128)(2,1)} %get-tuple-element.37), channel_id=1, source_target_pairs={{0,4},{4,8},{8,12},{12,16},{16,20},{20,24},{24,28},{28,32},{32,36}... | collective-permute-start | bytes 147464 | tf_op jit(solution)/shard_map/ppermute | solution.py:21
  192.1 5.4 collective-permute-start.5
  201.5 143.6 %all-reduce.23.cloned.1.call-start = ((), (), s32[]{:S(2)}) async-start(), calls=%async_computation.4 | async-start | bytes 786432 | tf_op jit(solution)/shard_map/psum | solution.py:54
  270.4 9.0 %collective-permute-start.6 = (bf16[96,1,256]{2,0,1:T(8,128)(2,1)S(1)}, bf16[96,1,256]{2,0,1:T(8,128)(2,1)S(1)}, u32[]{:S(2)}, u32[]{:S(2)}) collective-permute-start(bf16[96,1,256]{2,0,1:T(8,128)(2,1)S(1)} %get-tuple-element.35), channel_id=1, source_target_pairs={{0,4},{4,8},{8,12},{12,16},{16,20},{20,24},{24,28},{28,32},{32,36}... | collective-permute-start | bytes 147464 | tf_op jit(solution)/shard_map/ppermute | solution.py:21
  277.3 5.4 collective-permute-start.7
  286.1 143.4 %all-reduce.25.cloned.1.call-start = ((), (), s32[]{:S(2)}) async-start(), calls=%async_computation.5 | async-start | bytes 786432 | tf_op jit(solution)/shard_map/psum | solution.py:54
  354.9 9.2 %collective-permute-start.8 = (bf16[96,1,256]{2,0,1:T(8,128)(2,1)S(1)}, bf16[96,1,256]{2,0,1:T(8,128)(2,1)S(1)}, u32[]{:S(2)}, u32[]{:S(2)}) collective-permute-start(bf16[96,1,256]{2,0,1:T(8,128)(2,1)S(1)} %get-tuple-element.33), channel_id=1, source_target_pairs={{0,4},{4,8},{8,12},{12,16},{16,20},{20,24},{24,28},{28,32},{32,36}... | collective-permute-start | bytes 147464 | tf_op jit(solution)/shard_map/ppermute | solution.py:21
  361.8 5.4 collective-permute-start.9
  370.6 143.4 %all-reduce.27.cloned.1.call-start = ((), (), s32[]{:S(2)}) async-start(), calls=%async_computation.6 | async-start | bytes 786432 | tf_op jit(solution)/shard_map/psum | solution.py:54
  439.4 9.0 %collective-permute-start.10 = (bf16[96,1,256]{2,0,1:T(8,128)(2,1)S(1)}, bf16[96,1,256]{2,0,1:T(8,128)(2,1)S(1)}, u32[]{:S(2)}, u32[]{:S(2)}) collective-permute-start(bf16[96,1,256]{2,0,1:T(8,128)(2,1)S(1)} %get-tuple-element.31), channel_id=1, source_target_pairs={{0,4},{4,8},{8,12},{12,16},{16,20},{20,24},{24,28},{28,32},{32,36}... | collective-permute-start | bytes 147464 | tf_op jit(solution)/shard_map/ppermute | solution.py:21
  446.4 5.4 collective-permute-start.11
  455.1 143.3 %all-reduce.29.cloned.1.call-start = ((), (), s32[]{:S(2)}) async-start(), calls=%async_computation.7 | async-start | bytes 786432 | tf_op jit(solution)/shard_map/psum | solution.py:54
  523.7 9.0 %collective-permute-start.12 = (bf16[96,1,256]{2,0,1:T(8,128)(2,1)S(1)}, bf16[96,1,256]{2,0,1:T(8,128)(2,1)S(1)}, u32[]{:S(2)}, u32[]{:S(2)}) collective-permute-start(bf16[96,1,256]{2,0,1:T(8,128)(2,1)S(1)} %get-tuple-element.29), channel_id=1, source_target_pairs={{0,4},{4,8},{8,12},{12,16},{16,20},{20,24},{24,28},{28,32},{32,36}... | collective-permute-start | bytes 147464 | tf_op jit(solution)/shard_map/ppermute | solution.py:21
  530.7 5.4 collective-permute-start.13
  539.4 164.7 %all-reduce.31.cloned.1.call-start = ((), (), s32[]{:S(2)}) async-start(), calls=%async_computation.8 | async-start | bytes 1572864 | tf_op jit(solution)/shard_map/psum | solution.py:67
  599.6 8.0 %collective-permute-start.14 = (bf16[96,1,256]{2,0,1:T(8,128)(2,1)S(1)}, bf16[96,1,256]{2,0,1:T(8,128)(2,1)S(1)}, u32[]{:S(2)}, u32[]{:S(2)}) collective-permute-start(bf16[96,1,256]{2,0,1:T(8,128)(2,1)S(1)} %get-tuple-element.27), channel_id=1, source_target_pairs={{0,4},{4,8},{8,12},{12,16},{16,20},{20,24},{24,28},{28,32},{32,36}... | collective-permute-start | bytes 147464 | tf_op jit(solution)/shard_map/ppermute | solution.py:21
  605.5 5.4 collective-permute-start.15
  (19 other events, 1768.4 us)
Sparse Core Ops, SparseCore 0:
  30.7 59.7 all-reduce.16
  116.3 58.4 all-reduce.18
  201.7 58.8 all-reduce.20
  286.2 58.8 all-reduce.22
  370.7 58.7 all-reduce.24
  455.2 58.7 all-reduce.26
  539.6 58.7 all-reduce.28
  637.4 66.6 all-reduce.30
where the time goes:
time: 714 us; the launch traced here: 713 us
  waiting for transfers between devices  500 us (70%)
  starting transfers between devices  68.8 us (10%)
  blocking collectives  61.6 us (9%)
  local copies, waits for them, and re-layouts  42.9 us (6%)
  between operations  14.8 us (2%)
  other arithmetic  13.2 us (2%)
  matrix products  11.9 us (2%)
    psum x7, waiting for transfers between devices, conv_block(): lax.psum(contract(flat_weight, columns).astype(jnp.bfloat16), 'chan')  411 us
    psum x1, waiting for transfers between devices, up_block(): lax.psum(contract(flat_weight, columns).astype(jnp.bfloat16), 'chan')  66.8 us
    ppermute x8, starting transfers between devices, padded_2(): before = lax.ppermute(last, axis, up)  52.7 us
    psum x6, blocking collectives, rms_norm(): totals = lax.psum(squares, 'chan')  49.3 us
    ppermute x8, waiting for transfers between devices, padded_2(): after = lax.ppermute(first, axis, down)  21.9 us
    another operation x16, local copies, waits for them, and re-layouts, gather_columns(): return jnp.stack(shifted, 0).reshape(9 * chans, height * width)  17.3 us
    ppermute x8, starting transfers between devices, padded_2(): after = lax.ppermute(first, axis, down)  15.8 us
    unnamed x91, local copies, waits for them, and re-layouts  15 us
  transfers between devices with their start and end apart: 24, of which 15 were waited for; matrix products, arithmetic and copies ran while one was open for 1% of the time, Pallas kernels for 0%

commit v1 on v0

v1 whole, which is shorter than its diff:
```python
import jax
import jax.numpy as jnp
from jax import lax
from jax.experimental import pallas as pl
from jax.experimental.pallas import tpu as pltpu
from jax.sharding import PartitionSpec as P

CH = 384
UP = 192
EPS = 1e-06
COLS = 80
NRES = 54
NPIECE = 63
LAG = 8
MESH = pl.DeviceIdType.MESH


def remote(src, dst, send_sem, recv_sem, device):
    return pltpu.make_async_remote_copy(
        src_ref=src,
        dst_ref=dst,
        send_sem=send_sem,
        recv_sem=recv_sem,
        device_id=device,
        device_id_type=MESH,
    )


def kernel(
    lat_in, win_in, ibias_in, gain_in, shift_in, wres_in, rbias_in, wup_in, ubias_in,
    out_ref,
    lat_buf, win_buf, ibias_buf, gain_buf, shift_buf, rbias_buf, ubias_buf,
    wbuf, ubuf, table, lrow, win, x3, hbuf, upx, obuf,
    lat_s, lat_r, small_s, small_r, loc, zs, xs, ys, ps, r1, r2, out_s, out_r,
):
    s = lax.axis_index("seq")
    c = lax.axis_index("chan")
    core = lax.rem(s, 2)
    x = lax.rem(lax.div(s, 2), 4)
    y = lax.rem(lax.div(s, 8), 8)
    zh = lax.div(s, 64)
    z = zh * 4 + c
    bx, by = lax.rem(x, 2), lax.rem(y, 2)
    partner = (s + 1 - 2 * core, c)

    def z_device(step):
        zz = lax.rem(z + 8 + step, 8)
        return (((lax.div(zz, 4) * 8 + y) * 4 + x) * 2 + core, lax.rem(zz, 4))

    def x_device(step):
        xx = lax.rem(x + 4 + step, 4)
        return (((zh * 8 + y) * 4 + xx) * 2 + core, c)

    def y_device(step):
        yy = lax.rem(y + 8 + step, 8)
        return (((zh * 8 + yy) * 4 + x) * 2 + core, c)

    barrier = pltpu.get_barrier_semaphore()
    others = []
    for ds in range(-4, 5):
        peer = lax.rem(s + 128 + ds, 128)
        for dc in range(4):
            if ds != 0 or dc != 0:
                others.append((peer, lax.rem(c + dc, 4)))
    for step in (-2, -1, 1, 2):
        others.append(z_device(step))
    for step in (-1, 1):
        others.append(x_device(step))
        others.append(y_device(step))
    for device in others:
        pl.semaphore_signal(barrier, inc=1, device_id=device, device_id_type=MESH)
    for k in range(6):
        pltpu.make_async_copy(
            wres_in.at[k // 2, k % 2], wbuf.at[k, :, pl.ds(c * 96, 96), :], loc.at[k]
        ).start()
    pltpu.make_async_copy(wup_in, ubuf.at[:, pl.ds(c * 96, 96), :], loc.at[6]).start()
    pl.semaphore_wait(barrier, len(others))

    def lat_copy(ds, dc):
        return remote(
            lat_in,
            lat_buf.at[4 * (4 - ds) + c],
            lat_s.at[(ds + 4) * 4 + dc],
            lat_r.at[4 * (4 - ds) + c],
            (lax.rem(s + 128 + ds, 128), lax.rem(c + dc, 4)),
        )

    lat_pairs = [(ds, dc) for ds in range(-4, 5) for dc in range(4) if ds != 0 or dc != 0]
    for ds, dc in lat_pairs:
        lat_copy(ds, dc).start()
    pltpu.make_async_copy(lat_in, lat_buf.at[16 + c], loc.at[7]).start()
    smalls = (
        (win_in, win_buf),
        (ibias_in, ibias_buf),
        (gain_in, gain_buf),
        (shift_in, shift_buf),
        (rbias_in, rbias_buf),
        (ubias_in, ubias_buf),
    )

    def small_copy(i, dc):
        src, dst = smalls[i]
        return remote(
            src, dst.at[c], small_s.at[i * 4 + dc], small_r.at[i * 4 + c], (s, lax.rem(c + dc, 4))
        )

    for i in range(6):
        for dc in range(1, 4):
            small_copy(i, dc).start()
        pltpu.make_async_copy(smalls[i][0], smalls[i][1].at[c], loc.at[8 + i]).start()

    def res_piece(v, quarter):
        k, g = lax.div(v, 9), lax.div(lax.rem(v, 9), 3)
        return wbuf.at[k, pl.ds(3 * g, 3), pl.ds(quarter * 96 + core * 48, 48), :]

    def up_piece(v, quarter):
        g = lax.div(v - NRES, 3)
        return ubuf.at[pl.ds(3 * g, 3), pl.ds(quarter * 96 + core * 48, 48), :]

    def source_copy(v, up):
        which = lax.rem(v, 3)
        far = 4 * lax.rem(lax.div(v, 12), 2) - 2
        target = z_device(jnp.where(which == 0, -1, jnp.where(which == 2, 1, far)))
        if up:
            src = wup_in.at[pl.ds(3 * lax.div(v - NRES, 3), 3), pl.ds(core * 48, 48), :]
            dst = up_piece(v, c)
        else:
            k, g = lax.div(v, 9), lax.div(lax.rem(v, 9), 3)
            src = wres_in.at[
                lax.div(k, 2), lax.rem(k, 2), pl.ds(3 * g, 3), pl.ds(core * 48, 48), :
            ]
            dst = res_piece(v, c)
        return remote(src, dst, zs.at[v], r1.at[v], target)

    def is_source(v):
        chi = lax.rem(v, 4)
        return (lax.rem(chi, 2) == bx) & (lax.div(chi, 2) == by)

    for up, lo, hi in ((False, 0, NRES), (True, NRES, NPIECE)):

        @pl.loop(lo, hi)
        def _(v):
            @pl.when(is_source(v))
            def _():
                source_copy(v, up).start()

    def parts_of(v, up):
        piece = (up_piece if up else res_piece)(v, lax.rem(c + 1 + lax.rem(v, 3), 4))
        turn = 2 * lax.rem(lax.div(v, 8), 2) - 1
        return (
            remote(piece, piece, xs.at[v], r1.at[v], x_device(turn)),
            remote(piece, piece, ys.at[v], r1.at[v], y_device(turn)),
            remote(piece, piece, ps.at[v], r2.at[v], partner),
        )

    def role_of(v):
        chi, y_first = lax.rem(v, 4), lax.rem(lax.div(v, 4), 2)
        rx = lax.rem(bx + lax.rem(chi, 2), 2)
        ry = lax.rem(by + lax.div(chi, 2), 2)
        first = jnp.where(y_first == 1, rx, ry)
        second = jnp.where(y_first == 1, ry, rx)
        return jnp.where(first == 1, 2, second), y_first

    def pass_on(v, phase, up):
        role, y_first = role_of(v)
        low, high = (NRES, NPIECE) if up else (0, NRES)

        @pl.when((v >= low) & (v < high) & (role == phase))
        def _():
            along_x, along_y, across = parts_of(v, up)
            along_x.wait_recv()
            if phase == 0:
                along_x.start()
                along_y.start()
            if phase == 1:

                @pl.when(y_first == 1)
                def _():
                    along_x.start()

                @pl.when(y_first == 0)
                def _():
                    along_y.start()

            across.start()

    def relay(t):
        for phase in range(3):
            for up in (False, True):
                pass_on(t + (3 * LAG) - LAG * phase - 3 * LAG, phase, up)

    def relays(lo, hi):
        @pl.loop(lo, hi)
        def _(t):
            relay(t)

    ready = 9 + 2 * LAG
    relays(0, 6)

    for i in range(6):
        for dc in range(1, 4):
            src, dst = smalls[i]
            peer = lax.rem(c + dc, 4)
            remote(
                src, dst.at[peer], small_s.at[i * 4 + dc], small_r.at[i * 4 + peer], (s, peer)
            ).wait_recv()
        pltpu.make_async_copy(smalls[i][0], smalls[i][1].at[c], loc.at[8 + i]).wait()
    for q in range(4):
        for i in range(6):
            at = pl.ds(96 * q, 96)
            table[pl.ds(i, 1), at] = gain_buf[q, i // 2, pl.ds(i % 2, 1), :]
            table[pl.ds(6 + i, 1), at] = shift_buf[q, i // 2, pl.ds(i % 2, 1), :]
            table[pl.ds(12 + i, 1), at] = rbias_buf[q, i // 2, pl.ds(i % 2, 1), :]
        table[pl.ds(18, 1), pl.ds(96 * q, 96)] = ibias_buf[q]
        table[pl.ds(19, 1), pl.ds(48 * q, 48)] = ubias_buf[q]
    total = jnp.zeros((144, CH), jnp.float32)
    for q in range(4):
        row = lax.broadcasted_iota(jnp.int32, (144, 36), 0)
        col = lax.broadcasted_iota(jnp.int32, (144, 36), 1)
        put = (row == (col >> 2) * 16 + 4 * q + (col & 3)).astype(jnp.float32)
        total += jnp.dot(
            put.astype(jnp.bfloat16), win_buf[q], preferred_element_type=jnp.float32
        )
    win[...] = total.astype(jnp.bfloat16)

    for ds, dc in lat_pairs:
        slot = 4 * (4 - ds) + lax.rem(c + dc, 4)
        remote(lat_in, lat_buf.at[slot], lat_s.at[0], lat_r.at[slot], partner).wait_recv()
    pltpu.make_async_copy(lat_in, lat_buf.at[16 + c], loc.at[7]).wait()
    col_lo = jnp.maximum(8 - 64 * c, 0)
    col_hi = jnp.minimum(264 - 64 * c, COLS)
    turn = lax.rem(8 + 256 - 64 * c, 256)
    lane = lax.broadcasted_iota(jnp.int32, (16, 128), 1)

    @pl.loop(0, 18)
    def _(r):
        both = jnp.concatenate([lat_buf[2 * r], lat_buf[2 * r + 1]], axis=1).astype(jnp.float32)
        window = pltpu.roll(both, turn, 1)[:, :128]
        row = 2 * s - 8 + r
        top = jnp.where((row >= 0) & (row < 256), col_hi, 0)
        window = jnp.where((lane >= col_lo) & (lane < top), window, 0.0)
        at = pl.ds(pl.multiple_of(r * 16, 16), 16)
        lrow[0, at, :] = pltpu.roll(window, 1, 1).astype(jnp.bfloat16)
        lrow[1, at, :] = window.astype(jnp.bfloat16)
        lrow[2, at, :] = pltpu.roll(window, 127, 1).astype(jnp.bfloat16)

    pixel = lax.broadcasted_iota(jnp.int32, (COLS, CH), 0)

    def spread(dst, a, values):
        row = 2 * s - 7 + a
        top = jnp.where((row >= 0) & (row < 256), col_hi, 0)
        kept = jnp.where((pixel >= col_lo) & (pixel < top), values, 0.0)
        x3[dst, a, :, pl.ds(0, CH)] = pltpu.roll(kept, 1, 0).astype(jnp.bfloat16)
        x3[dst, a, :, pl.ds(CH, CH)] = kept.astype(jnp.bfloat16)
        x3[dst, a, :, pl.ds(2 * CH, CH)] = pltpu.roll(kept, COLS - 1, 0).astype(jnp.bfloat16)

    def normed(values, i):
        mean = jnp.sum(values * values, axis=1, keepdims=True) * (1.0 / CH)
        u = values * lax.rsqrt(mean + EPS) * table[pl.ds(i, 1), :] + table[pl.ds(6 + i, 1), :]
        half = 0.5 * u
        return half * jnp.tanh(half) + half

    def rounded(values):
        return values.astype(jnp.bfloat16).astype(jnp.float32)

    @pl.loop(0, 16)
    def _(i):
        columns = jnp.concatenate(
            [
                lrow[q, pl.ds(pl.multiple_of((i + p) * 16, 16), 16), :]
                for p in range(3)
                for q in range(3)
            ],
            axis=0,
        )
        acc = lax.dot_general(
            columns, win[...], (((0,), (0,)), ((), ())), preferred_element_type=jnp.float32
        )
        stream = rounded(acc[:COLS] + table[pl.ds(18, 1), :])
        hbuf[i] = stream
        spread(0, i, normed(stream, 0))
        relays(6 + lax.div(i * (ready - 6), 16), 6 + lax.div((i + 1) * (ready - 6), 16))

    for k in range(6):
        src, dst = k % 2, 1 - k % 2
        pltpu.make_async_copy(
            wres_in.at[k // 2, k % 2], wbuf.at[k, :, pl.ds(c * 96, 96), :], loc.at[k]
        ).wait()

        @pl.loop(9 * k, 9 * k + 9)
        def _(v):
            piece = wbuf.at[k, pl.ds(3 * lax.div(lax.rem(v, 9), 3), 3),
                            pl.ds(lax.rem(c + 1 + lax.rem(v, 3), 4) * 96 + (1 - core) * 48, 48), :]
            remote(piece, piece, ps.at[v], r2.at[v], partner).wait_recv()

        blocks = 7 - k

        @pl.loop(0, blocks)
        def _(b):
            a = k + 1 + 2 * b
            acc = jnp.zeros((2 * COLS, CH), jnp.float32)
            for p in range(3):
                acc += jnp.dot(
                    x3[src, pl.ds(a - 1 + p, 2)].reshape(2 * COLS, 3 * CH),
                    wbuf[k, pl.ds(3 * p, 3)].reshape(3 * CH, CH),
                    preferred_element_type=jnp.float32,
                )
            acc += table[pl.ds(12 + k, 1), :]
            for j in range(2):
                values = acc[j * COLS : (j + 1) * COLS]
                if k % 2 == 0:
                    spread(dst, a + j, normed(values, k + 1))
                else:
                    values = rounded(hbuf[a + j] + values)
                    hbuf[a + j] = values
                    spread(dst, a + j, normed(values, k + 1) if k < 5 else values)
            relays(ready + 9 * k + lax.div(b * 9, blocks), ready + 9 * k + lax.div((b + 1) * 9, blocks))

    pltpu.make_async_copy(wup_in, ubuf.at[:, pl.ds(c * 96, 96), :], loc.at[6]).wait()

    @pl.loop(NRES, NPIECE)
    def _(v):
        piece = ubuf.at[pl.ds(3 * lax.div(v - NRES, 3), 3),
                        pl.ds(lax.rem(c + 1 + lax.rem(v, 3), 4) * 96 + (1 - core) * 48, 48), :]
        remote(piece, piece, ps.at[v], r2.at[v], partner).wait_recv()

    def out_copy(r, dc):
        peer = lax.rem(c + dc, 4)
        return remote(
            obuf.at[r, pl.ds(peer * 48, 48), :],
            out_ref.at[r, :, pl.ds(c * 128, 128)],
            out_s.at[r * 4 + dc],
            out_r.at[r * 4 + c],
            (s, peer),
        )

    lanes = ((0, 1, 1), (1, 1, 2))
    rows = ((-1, 0, 0), (0, 0, 1))
    for i in range(2):
        for b2 in range(2):
            acc = jnp.zeros((2 * COLS, UP), jnp.float32)
            for p in range(3):
                lhs = jnp.concatenate(
                    [
                        jnp.concatenate(
                            [
                                x3[0, 7 + i + rows[a2][p], :, pl.ds(CH * lanes[b2][q], CH)]
                                for q in range(3)
                            ],
                            axis=1,
                        )
                        for a2 in range(2)
                    ],
                    axis=0,
                )
                acc += jnp.dot(
                    lhs,
                    ubuf[pl.ds(3 * p, 3)].reshape(3 * CH, UP),
                    preferred_element_type=jnp.float32,
                )
            acc += table[pl.ds(19, 1), pl.ds(0, UP)]
            for a2 in range(2):
                part = acc[a2 * COLS + 8 : a2 * COLS + 72]
                upx[a2, 0, pl.ds(b2, 64, stride=2), :] = part[:, :128]
                upx[a2, 1, pl.ds(b2, 64, stride=2), pl.ds(0, 64)] = part[:, 128:]
        for a2 in range(2):
            r = 2 * i + a2
            obuf[r, pl.ds(0, 128), :] = upx[a2, 0].T.astype(jnp.bfloat16)
            obuf[r, pl.ds(128, 64), :] = upx[a2, 1].T[:64].astype(jnp.bfloat16)
            for dc in range(1, 4):
                out_copy(r, dc).start()
            pltpu.make_async_copy(
                obuf.at[r, pl.ds(c * 48, 48), :],
                out_ref.at[r, :, pl.ds(c * 128, 128)],
                loc.at[14 + r],
            ).start()

    for r in range(4):
        for dc in range(1, 4):
            out_copy(r, dc).wait_send()
            peer = lax.rem(c + dc, 4)
            remote(
                obuf.at[r, pl.ds(0, 48), :],
                out_ref.at[r, :, pl.ds(peer * 128, 128)],
                out_s.at[r * 4 + dc],
                out_r.at[r * 4 + peer],
                (s, peer),
            ).wait_recv()
        pltpu.make_async_copy(
            obuf.at[r, pl.ds(c * 48, 48), :],
            out_ref.at[r, :, pl.ds(c * 128, 128)],
            loc.at[14 + r],
        ).wait()
    for ds, dc in lat_pairs:
        lat_copy(ds, dc).wait_send()
    for i in range(6):
        for dc in range(1, 4):
            small_copy(i, dc).wait_send()
    for up, lo, hi in ((False, 0, NRES), (True, NRES, NPIECE)):

        @pl.loop(lo, hi)
        def _(v):
            @pl.when(is_source(v))
            def _():
                source_copy(v, up).wait_send()

            role, y_first = role_of(v)
            along_x, along_y, across = parts_of(v, up)

            @pl.when((role == 0) | ((role == 1) & (y_first == 1)))
            def _():
                along_x.wait_send()

            @pl.when((role == 0) | ((role == 1) & (y_first == 0)))
            def _():
                along_y.wait_send()

            across.wait_send()


def body(
    latent, in_weight, in_bias, norm_gain, norm_shift, res_weight, res_bias, up_weight, up_bias
):
    bf16, f32 = jnp.bfloat16, jnp.float32
    dma = pltpu.SemaphoreType.DMA
    image = pl.pallas_call(
        kernel,
        out_shape=jax.ShapeDtypeStruct((4, 48, 512), bf16),
        in_specs=[pl.BlockSpec(memory_space=pl.ANY)] * 9,
        out_specs=pl.BlockSpec(memory_space=pltpu.VMEM),
        scratch_shapes=[
            pltpu.VMEM((36, 16, 128), bf16),
            pltpu.VMEM((4, 36, CH), bf16),
            pltpu.VMEM((4, 1, 96), f32),
            pltpu.VMEM((4, 3, 2, 96), f32),
            pltpu.VMEM((4, 3, 2, 96), f32),
            pltpu.VMEM((4, 3, 2, 96), f32),
            pltpu.VMEM((4, 1, 48), f32),
            pltpu.VMEM((6, 9, CH, CH), bf16),
            pltpu.VMEM((9, CH, UP), bf16),
            pltpu.VMEM((24, CH), f32),
            pltpu.VMEM((3, 288, 128), bf16),
            pltpu.VMEM((144, CH), bf16),
            pltpu.VMEM((2, 16, COLS, 3 * CH), bf16),
            pltpu.VMEM((16, COLS, CH), f32),
            pltpu.VMEM((2, 2, 128, 128), f32),
            pltpu.VMEM((4, UP, 128), bf16),
            dma((36,)),
            dma((36,)),
            dma((24,)),
            dma((24,)),
            dma((18,)),
            dma((NPIECE,)),
            dma((NPIECE,)),
            dma((NPIECE,)),
            dma((NPIECE,)),
            dma((NPIECE,)),
            dma((NPIECE,)),
            dma((16,)),
            dma((16,)),
        ],
        compiler_params=pltpu.CompilerParams(
            collective_id=0, has_side_effects=True, vmem_limit_bytes=60 << 20
        ),
    )(
        latent.T,
        in_weight.reshape(36, CH),
        in_bias[None],
        norm_gain,
        norm_shift,
        res_weight,
        res_bias,
        up_weight,
        up_bias[None],
    )
    return image.transpose(1, 0, 2)


def solution(mesh):
    placed = (
        P(("seq", "chan"), None),
        P(None, "chan", None),
        P("chan"),
        P(None, None, "chan"),
        P(None, None, "chan"),
        P(None, None, None, "chan", None),
        P(None, None, "chan"),
        P(None, "chan", None),
        P("chan"),
    )
    return jax.shard_map(
        body, mesh=mesh, in_specs=placed, out_specs=P("chan", "seq", None), check_vma=False
    )
```

time: 714 us -> 105 us (0.15)
  waiting for transfers between devices: 500 us -> 0 us
  Pallas kernels: 0 us -> 101 us
  starting transfers between devices: 68.8 us -> 0 us
  blocking collectives: 61.6 us -> 0 us
  local copies, waits for them, and re-layouts: 42.9 us -> 3.14 us
  between operations: 14.8 us -> 0.01 us
  other arithmetic: 13.2 us -> 0 us
  matrix products: 11.9 us -> 0 us
    psum x8 -> x0, waiting for transfers between devices: 478 us -> none  [the longest x7 411 us: conv_block(): lax.psum(contract(flat_weight, columns).astype(jnp.bfloat16), 'chan')]
    pallas_call x0 -> x1, Pallas kernels: none -> 101 us  [body(): pl.pallas_call(kernel, out_shape=jax.ShapeDtypeStruct((4, 48, 512), bf16)...]
    ppermute x16 -> x0, starting transfers between devices: 68.5 us -> none  [the longest x8 52.7 us: padded_2(): before = lax.ppermute(last, axis, up)]
    psum x6 -> x0, blocking collectives: 49.3 us -> none  [rms_norm(): totals = lax.psum(squares, 'chan')]
    ppermute x16 -> x0, waiting for transfers between devices: 21.9 us -> none  [the longest x8 21.9 us: padded_2(): after = lax.ppermute(first, axis, down)]
    another operation x16 -> x0, local copies, waits for them, and re-layouts: 17.3 us -> none  [gather_columns(): return jnp.stack(shifted, 0).reshape(9 * chans, height * width)]
    unnamed x91 -> x0, local copies, waits for them, and re-layouts: 15 us -> none
    all_to_all x1 -> x0, blocking collectives: 12.4 us -> none  [body(): lax.all_to_all(latent, 'chan', split_axis=1, concat_axis=0, tiled=True)]
  transfers between devices with their start and end apart: 24 -> 0, of which waited for: 15 -> 0; matrix products, arithmetic and copies ran while one was open for 1% -> 0% of each run, Pallas kernels for 0% -> 0%
where the time goes in v1:
time: 105 us; the launch traced here: 104 us
  Pallas kernels  101 us (96%)
  local copies, waits for them, and re-layouts  3.14 us (3%)
    pallas_call x1, Pallas kernels, body(): pl.pallas_call(kernel, out_shape=jax.ShapeDtypeStruct((4, 48, 512), bf16)...  101 us

profile of v1, /device:TPU:1, one launch (start us, length us, event | category | flops | bytes accessed | tf_op | source)
XLA Modules:
  0.0 104.4 jit_solution(13714109869351201975)
XLA Ops:
  0.0 1.4 %reshape.3.win_in = bf16[36,384]{1,0:T(8,128)(2,1)} reshape(bf16[9,4,384]{2,1,0:T(4,128)(2,1)} %param.10) | data formatting | bytes 55296 | tf_op jit(solution)/shard_map/reshape | solution.py:467
  1.4 101.2 %shard_map.91 = bf16[4,48,512]{2,1,0:T(8,128)(2,1)} custom-call(bf16[16,128]{1,0:T(8,128)(2,1)} %bitcast.5, bf16[36,384]{1,0:T(8,128)(2,1)} %reshape.3.win_in, f32[1,96]{1,0:T(1,128)} %bitcast.6, f32[3,2,96]{2,1,0:T(2,128)} %gain_in.1, f32[3,2,96]{2,1,0:T(2,128)} %shift_in.1, bf16[3,2,9,96,384]{4,3,2,1,0:T(8,128)(2,1)} %wres_in.1, f32[3,2,96]{2,1,0:T(2,128)} %rbias_in.1, ...), custom_call_target="tpu_custom_call" | custom-call | tf_op jit(solution)/shard_map/pallas_call | solution.py:426
  102.6 1.8 %copy.10 = bf16[48,4,512]{2,1,0:T(4,128)(2,1)} copy(bf16[48,4,512]{2,0,1:T(8,128)(2,1)} %bitcast.4) | data formatting | bytes 393216 | tf_op jit(solution)/shard_map/transpose | solution.py:476

commit v2 on v1

--- a/solution.py
+++ b/solution.py
@@ -11,7 +11,9 @@
 COLS = 80
 NRES = 54
 NPIECE = 63
-LAG = 8
+LAG = 14
+SHORT = frozenset(range(45, 63))
+FIRST = 12
 MESH = pl.DeviceIdType.MESH
 
 
@@ -30,7 +32,7 @@
     lat_in, win_in, ibias_in, gain_in, shift_in, wres_in, rbias_in, wup_in, ubias_in,
     out_ref,
     lat_buf, win_buf, ibias_buf, gain_buf, shift_buf, rbias_buf, ubias_buf,
-    wbuf, ubuf, table, lrow, win, x3, hbuf, upx, obuf,
+    wbuf, ubuf, table, lrow, wide, win, x3, hbuf, acc, upx, obuf,
     lat_s, lat_r, small_s, small_r, loc, zs, xs, ys, ps, r1, r2, out_s, out_r,
 ):
     s = lax.axis_index("seq")
@@ -109,93 +111,92 @@
             small_copy(i, dc).start()
         pltpu.make_async_copy(smalls[i][0], smalls[i][1].at[c], loc.at[8 + i]).start()
 
-    def res_piece(v, quarter):
-        k, g = lax.div(v, 9), lax.div(lax.rem(v, 9), 3)
-        return wbuf.at[k, pl.ds(3 * g, 3), pl.ds(quarter * 96 + core * 48, 48), :]
-
-    def up_piece(v, quarter):
-        g = lax.div(v - NRES, 3)
-        return ubuf.at[pl.ds(3 * g, 3), pl.ds(quarter * 96 + core * 48, 48), :]
-
-    def source_copy(v, up):
-        which = lax.rem(v, 3)
-        far = 4 * lax.rem(lax.div(v, 12), 2) - 2
-        target = z_device(jnp.where(which == 0, -1, jnp.where(which == 2, 1, far)))
-        if up:
-            src = wup_in.at[pl.ds(3 * lax.div(v - NRES, 3), 3), pl.ds(core * 48, 48), :]
-            dst = up_piece(v, c)
+    sign = 1 - 2 * core
+    hops = {step: z_device(step * sign) for step in (-2, -1, 1, 2)}
+    aside = {step: x_device(step * sign) for step in (-1, 1)}
+    along = {step: y_device(step * sign) for step in (-1, 1)}
+    mine = [lax.rem(c + 4 + q * sign, 4) * 96 + core * 48 for q in range(4)]
+    theirs = [lax.rem(c + 4 - q * sign, 4) * 96 + (1 - core) * 48 for q in range(4)]
+
+    def piece_at(v, row):
+        if v < NRES:
+            return wbuf.at[v // 9, pl.ds(v % 9 // 3 * 3, 3), pl.ds(row, 48), :]
+        return ubuf.at[pl.ds((v - NRES) // 3 * 3, 3), pl.ds(row, 48), :]
+
+    def source_copy(v):
+        step = (-1, 4 * (v // 12 % 2) - 2, 1)[v % 3]
+        rows = pl.ds(core * 48, 48)
+        if v < NRES:
+            src = wres_in.at[v // 18, v // 9 % 2, pl.ds(v % 9 // 3 * 3, 3), rows, :]
         else:
-            k, g = lax.div(v, 9), lax.div(lax.rem(v, 9), 3)
-            src = wres_in.at[
-                lax.div(k, 2), lax.rem(k, 2), pl.ds(3 * g, 3), pl.ds(core * 48, 48), :
-            ]
-            dst = res_piece(v, c)
-        return remote(src, dst, zs.at[v], r1.at[v], target)
+            src = wup_in.at[pl.ds((v - NRES) // 3 * 3, 3), rows, :]
+        return remote(src, piece_at(v, mine[0]), zs.at[v], r1.at[v], hops[step])
+
+    def is_colour(i):
+        return (bx == i % 2) & (by == i // 2)
+
+    def x_is_last(v):
+        return v // 4 % 2 == 1
 
     def is_source(v):
-        chi = lax.rem(v, 4)
-        return (lax.rem(chi, 2) == bx) & (lax.div(chi, 2) == by)
-
-    for up, lo, hi in ((False, 0, NRES), (True, NRES, NPIECE)):
-
-        @pl.loop(lo, hi)
-        def _(v):
-            @pl.when(is_source(v))
-            def _():
-                source_copy(v, up).start()
-
-    def parts_of(v, up):
-        piece = (up_piece if up else res_piece)(v, lax.rem(c + 1 + lax.rem(v, 3), 4))
-        turn = 2 * lax.rem(lax.div(v, 8), 2) - 1
-        return (
-            remote(piece, piece, xs.at[v], r1.at[v], x_device(turn)),
-            remote(piece, piece, ys.at[v], r1.at[v], y_device(turn)),
-            remote(piece, piece, ps.at[v], r2.at[v], partner),
-        )
-
-    def role_of(v):
-        chi, y_first = lax.rem(v, 4), lax.rem(lax.div(v, 4), 2)
-        rx = lax.rem(bx + lax.rem(chi, 2), 2)
-        ry = lax.rem(by + lax.div(chi, 2), 2)
-        first = jnp.where(y_first == 1, rx, ry)
-        second = jnp.where(y_first == 1, ry, rx)
-        return jnp.where(first == 1, 2, second), y_first
-
-    def pass_on(v, phase, up):
-        role, y_first = role_of(v)
-        low, high = (NRES, NPIECE) if up else (0, NRES)
-
-        @pl.when((v >= low) & (v < high) & (role == phase))
+        if v in SHORT:
+            return bx == v % 2 if x_is_last(v) else by == v // 2 % 2
+        return is_colour(v % 4)
+
+    for v in range(NPIECE):
+
+        @pl.when(is_source(v))
         def _():
-            along_x, along_y, across = parts_of(v, up)
-            along_x.wait_recv()
-            if phase == 0:
-                along_x.start()
-                along_y.start()
-            if phase == 1:
-
-                @pl.when(y_first == 1)
-                def _():
-                    along_x.start()
-
-                @pl.when(y_first == 0)
-                def _():
-                    along_y.start()
-
-            across.start()
+            source_copy(v).start()
+
+    def x_copy(v):
+        piece = piece_at(v, mine[1 + v % 3])
+        return remote(piece, piece, xs.at[v], r1.at[v], aside[2 * (v // 8 % 2) - 1])
+
+    def y_copy(v):
+        piece = piece_at(v, mine[1 + v % 3])
+        return remote(piece, piece, ys.at[v], r1.at[v], along[2 * (v // 8 % 2) - 1])
+
+    def core_copy(v):
+        piece = piece_at(v, mine[1 + v % 3])
+        return remote(piece, piece, ps.at[v], r2.at[v], partner)
+
+    def phases(v):
+        final = x_copy if x_is_last(v) else y_copy
+        rest = bx != v % 2 if x_is_last(v) else by != v // 2 % 2
+        if v in SHORT:
+            return ((is_source(v), (final,)), (rest, ()))
+        second = is_colour(v % 4 ^ (2 if x_is_last(v) else 1))
+        return ((is_source(v), (x_copy, y_copy)), (second, (final,)), (rest, ()))
+
+    def length(v):
+        return 2 if v in SHORT else 3
 
     def relay(t):
         for phase in range(3):
-            for up in (False, True):
-                pass_on(t + (3 * LAG) - LAG * phase - 3 * LAG, phase, up)
+            v = t - LAG * phase
+            if 0 <= v < NPIECE and phase < length(v):
+                reached, onward = phases(v)[phase]
+
+                @pl.when(reached)
+                def _():
+                    x_copy(v).wait_recv()
+                    for copy in onward:
+                        copy(v).start()
+                    core_copy(v).start()
 
     def relays(lo, hi):
-        @pl.loop(lo, hi)
-        def _(t):
+        for t in range(lo, hi):
             relay(t)
 
-    ready = 9 + 2 * LAG
-    relays(0, 6)
+    def arrived(v):
+        piece = piece_at(v, theirs[1 + v % 3])
+        remote(piece, piece, ps.at[v], r2.at[v], partner).wait_recv()
+
+    need = [
+        1 + max(v + LAG * (length(v) - 1) for v in range(9 * k + 9)) for k in range(7)
+    ]
+    relays(0, FIRST)
 
     for i in range(6):
         for dc in range(1, 4):
@@ -213,15 +214,10 @@
             table[pl.ds(12 + i, 1), at] = rbias_buf[q, i // 2, pl.ds(i % 2, 1), :]
         table[pl.ds(18, 1), pl.ds(96 * q, 96)] = ibias_buf[q]
         table[pl.ds(19, 1), pl.ds(48 * q, 48)] = ubias_buf[q]
-    total = jnp.zeros((144, CH), jnp.float32)
     for q in range(4):
-        row = lax.broadcasted_iota(jnp.int32, (144, 36), 0)
-        col = lax.broadcasted_iota(jnp.int32, (144, 36), 1)
-        put = (row == (col >> 2) * 16 + 4 * q + (col & 3)).astype(jnp.float32)
-        total += jnp.dot(
-            put.astype(jnp.bfloat16), win_buf[q], preferred_element_type=jnp.float32
-        )
-    win[...] = total.astype(jnp.bfloat16)
+        for t in range(9):
+            wide[pl.ds(16 * t + 4 * q, 4), :] = win_buf[q, t].astype(jnp.float32)
+    win[...] = wide[...].astype(jnp.bfloat16)
 
     for ds, dc in lat_pairs:
         slot = 4 * (4 - ds) + lax.rem(c + dc, 4)
@@ -263,8 +259,7 @@
     def rounded(values):
         return values.astype(jnp.bfloat16).astype(jnp.float32)
 
-    @pl.loop(0, 16)
-    def _(i):
+    def first_conv(i):
         columns = jnp.concatenate(
             [
                 lrow[q, pl.ds(pl.multiple_of((i + p) * 16, 16), 16), :]
@@ -273,13 +268,16 @@
             ],
             axis=0,
         )
-        acc = lax.dot_general(
+        product = lax.dot_general(
             columns, win[...], (((0,), (0,)), ((), ())), preferred_element_type=jnp.float32
         )
-        stream = rounded(acc[:COLS] + table[pl.ds(18, 1), :])
+        stream = rounded(product[:COLS] + table[pl.ds(18, 1), :])
         hbuf[i] = stream
         spread(0, i, normed(stream, 0))
-        relays(6 + lax.div(i * (ready - 6), 16), 6 + lax.div((i + 1) * (ready - 6), 16))
+
+    for part in range(4):
+        pl.loop(4 * part, 4 * part + 4)(first_conv)
+        relays(FIRST + part * (need[0] - FIRST) // 4, FIRST + (part + 1) * (need[0] - FIRST) // 4)
 
     for k in range(6):
         src, dst = k % 2, 1 - k % 2
@@ -287,42 +285,51 @@
             wres_in.at[k // 2, k % 2], wbuf.at[k, :, pl.ds(c * 96, 96), :], loc.at[k]
         ).wait()
 
-        @pl.loop(9 * k, 9 * k + 9)
-        def _(v):
-            piece = wbuf.at[k, pl.ds(3 * lax.div(lax.rem(v, 9), 3), 3),
-                            pl.ds(lax.rem(c + 1 + lax.rem(v, 3), 4) * 96 + (1 - core) * 48, 48), :]
-            remote(piece, piece, ps.at[v], r2.at[v], partner).wait_recv()
-
-        blocks = 7 - k
-
-        @pl.loop(0, blocks)
+        for v in range(9 * k, 9 * k + 9):
+            arrived(v)
+        height = 7 - k
+        done, steps = need[k], need[k + 1] - need[k]
+
+        @pl.loop(0, 2)
         def _(b):
-            a = k + 1 + 2 * b
-            acc = jnp.zeros((2 * COLS, CH), jnp.float32)
+            a = k + 1 + height * b
+            sums = acc.at[pl.ds(0, height * COLS)]
+
+            def keep_on(p):
+                for part in range(2):
+
+                    @pl.when(b == part)
+                    def _():
+                        at = 3 * part + p
+                        relays(done + steps * at // 6, done + steps * (at + 1) // 6)
+
             for p in range(3):
-                acc += jnp.dot(
-                    x3[src, pl.ds(a - 1 + p, 2)].reshape(2 * COLS, 3 * CH),
+                term = jnp.dot(
+                    x3[src, pl.ds(a - 1 + p, height)].reshape(height * COLS, 3 * CH),
                     wbuf[k, pl.ds(3 * p, 3)].reshape(3 * CH, CH),
                     preferred_element_type=jnp.float32,
                 )
-            acc += table[pl.ds(12 + k, 1), :]
-            for j in range(2):
-                values = acc[j * COLS : (j + 1) * COLS]
+                if p == 0:
+                    sums[...] = term
+                elif p == 1:
+                    sums[...] += term
+                if p < 2:
+                    keep_on(p)
+            total = sums[...] + term + table[pl.ds(12 + k, 1), :]
+            for j in range(height):
+                values = total[j * COLS : (j + 1) * COLS]
                 if k % 2 == 0:
                     spread(dst, a + j, normed(values, k + 1))
                 else:
                     values = rounded(hbuf[a + j] + values)
                     hbuf[a + j] = values
                     spread(dst, a + j, normed(values, k + 1) if k < 5 else values)
-            relays(ready + 9 * k + lax.div(b * 9, blocks), ready + 9 * k + lax.div((b + 1) * 9, blocks))
+            keep_on(2)
 
     pltpu.make_async_copy(wup_in, ubuf.at[:, pl.ds(c * 96, 96), :], loc.at[6]).wait()
 
-    @pl.loop(NRES, NPIECE)
-    def _(v):
-        piece = ubuf.at[pl.ds(3 * lax.div(v - NRES, 3), 3),
-                        pl.ds(lax.rem(c + 1 + lax.rem(v, 3), 4) * 96 + (1 - core) * 48, 48), :]
-        remote(piece, piece, ps.at[v], r2.at[v], partner).wait_recv()
+    for v in range(NRES, NPIECE):
+        arrived(v)
 
     def out_copy(r, dc):
         peer = lax.rem(c + dc, 4)
@@ -338,7 +345,7 @@
     rows = ((-1, 0, 0), (0, 0, 1))
     for i in range(2):
         for b2 in range(2):
-            acc = jnp.zeros((2 * COLS, UP), jnp.float32)
+            grown = jnp.zeros((2 * COLS, UP), jnp.float32)
             for p in range(3):
                 lhs = jnp.concatenate(
                     [
@@ -353,14 +360,14 @@
                     ],
                     axis=0,
                 )
-                acc += jnp.dot(
+                grown += jnp.dot(
                     lhs,
                     ubuf[pl.ds(3 * p, 3)].reshape(3 * CH, UP),
                     preferred_element_type=jnp.float32,
                 )
-            acc += table[pl.ds(19, 1), pl.ds(0, UP)]
+            grown += table[pl.ds(19, 1), pl.ds(0, UP)]
             for a2 in range(2):
-                part = acc[a2 * COLS + 8 : a2 * COLS + 72]
+                part = grown[a2 * COLS + 8 : a2 * COLS + 72]
                 upx[a2, 0, pl.ds(b2, 64, stride=2), :] = part[:, :128]
                 upx[a2, 1, pl.ds(b2, 64, stride=2), pl.ds(0, 64)] = part[:, 128:]
         for a2 in range(2):
@@ -375,6 +382,25 @@
                 loc.at[14 + r],
             ).start()
 
+    for v in range(NPIECE):
+
+        @pl.when(is_source(v))
+        def _():
+            source_copy(v).wait_send()
+
+        for reached, onward in phases(v)[:-1]:
+
+            @pl.when(reached)
+            def _():
+                for copy in onward:
+                    copy(v).wait_send()
+
+        core_copy(v).wait_send()
+    for ds, dc in lat_pairs:
+        lat_copy(ds, dc).wait_send()
+    for i in range(6):
+        for dc in range(1, 4):
+            small_copy(i, dc).wait_send()
     for r in range(4):
         for dc in range(1, 4):
             out_copy(r, dc).wait_send()
@@ -391,31 +417,6 @@
             out_ref.at[r, :, pl.ds(c * 128, 128)],
             loc.at[14 + r],
         ).wait()
-    for ds, dc in lat_pairs:
-        lat_copy(ds, dc).wait_send()
-    for i in range(6):
-        for dc in range(1, 4):
-            small_copy(i, dc).wait_send()
-    for up, lo, hi in ((False, 0, NRES), (True, NRES, NPIECE)):
-
-        @pl.loop(lo, hi)
-        def _(v):
-            @pl.when(is_source(v))
-            def _():
-                source_copy(v, up).wait_send()
-
-            role, y_first = role_of(v)
-            along_x, along_y, across = parts_of(v, up)
-
-            @pl.when((role == 0) | ((role == 1) & (y_first == 1)))
-            def _():
-                along_x.wait_send()
-
-            @pl.when((role == 0) | ((role == 1) & (y_first == 0)))
-            def _():
-                along_y.wait_send()
-
-            across.wait_send()
 
 
 def body(
@@ -430,7 +431,7 @@
         out_specs=pl.BlockSpec(memory_space=pltpu.VMEM),
         scratch_shapes=[
             pltpu.VMEM((36, 16, 128), bf16),
-            pltpu.VMEM((4, 36, CH), bf16),
+            pltpu.VMEM((4, 9, 4, CH), bf16),
             pltpu.VMEM((4, 1, 96), f32),
             pltpu.VMEM((4, 3, 2, 96), f32),
             pltpu.VMEM((4, 3, 2, 96), f32),
@@ -440,9 +441,11 @@
             pltpu.VMEM((9, CH, UP), bf16),
             pltpu.VMEM((24, CH), f32),
             pltpu.VMEM((3, 288, 128), bf16),
+            pltpu.VMEM((144, CH), f32),
             pltpu.VMEM((144, CH), bf16),
             pltpu.VMEM((2, 16, COLS, 3 * CH), bf16),
             pltpu.VMEM((16, COLS, CH), f32),
+            pltpu.VMEM((7 * COLS, CH), f32),
             pltpu.VMEM((2, 2, 128, 128), f32),
             pltpu.VMEM((4, UP, 128), bf16),
             dma((36,)),
@@ -464,7 +467,7 @@
         ),
     )(
         latent.T,
-        in_weight.reshape(36, CH),
+        in_weight,
         in_bias[None],
         norm_gain,
         norm_shift,

time: 105 us -> 91.3 us (0.87)
  Pallas kernels: 101 us -> 89.4 us
  local copies, waits for them, and re-layouts: 3.14 us -> 1.76 us
    pallas_call x1, Pallas kernels: 101 us -> 89.4 us  [body(): pl.pallas_call(kernel, out_shape=jax.ShapeDtypeStruct((4, 48, 512), bf16)...]
    reshape x1 -> x0, local copies, waits for them, and re-layouts: 1.38 us -> none  [body(): in_weight.reshape(36, CH)]
where the time goes in v2:
time: 91.3 us; the launch traced here: 91.2 us
  Pallas kernels  89.4 us (98%)
  local copies, waits for them, and re-layouts  1.76 us (2%)
    pallas_call x1, Pallas kernels, body(): pl.pallas_call(kernel, out_shape=jax.ShapeDtypeStruct((4, 48, 512), bf16)...  89.4 us

profile of v2, /device:TPU:1, one launch (start us, length us, event | category | flops | bytes accessed | tf_op | source)
XLA Modules:
  0.0 91.2 jit_solution(14997606882796143065)
XLA Ops:
  0.0 89.4 %shard_map.91 = bf16[4,48,512]{2,1,0:T(8,128)(2,1)} custom-call(bf16[16,128]{1,0:T(8,128)(2,1)} %bitcast.5, bf16[9,4,384]{2,1,0:T(4,128)(2,1)} %win_in.1, f32[1,96]{1,0:T(1,128)} %bitcast.6, f32[3,2,96]{2,1,0:T(2,128)} %gain_in.1, f32[3,2,96]{2,1,0:T(2,128)} %shift_in.1, bf16[3,2,9,96,384]{4,3,2,1,0:T(8,128)(2,1)} %wres_in.1, f32[3,2,96]{2,1,0:T(2,128)} %rbias_in.1, ...), custom_call_target="tpu_custom_call" | custom-call | tf_op jit(solution)/shard_map/pallas_call | solution.py:427
  89.4 1.8 %copy.10 = bf16[48,4,512]{2,1,0:T(4,128)(2,1)} copy(bf16[48,4,512]{2,0,1:T(8,128)(2,1)} %bitcast.4) | data formatting | bytes 393216 | tf_op jit(solution)/shard_map/transpose | solution.py:479

commit v3 on v2

--- a/solution.py
+++ b/solution.py
@@ -11,9 +11,9 @@
 COLS = 80
 NRES = 54
 NPIECE = 63
-LAG = 14
+LAGS = tuple(min(14, 7 + v // 6) for v in range(63))
 SHORT = frozenset(range(45, 63))
-FIRST = 12
+FIRST = 10
 MESH = pl.DeviceIdType.MESH
 
 
@@ -174,8 +174,9 @@
 
     def relay(t):
         for phase in range(3):
-            v = t - LAG * phase
-            if 0 <= v < NPIECE and phase < length(v):
+            for v in range(NPIECE):
+                if v + LAGS[v] * phase != t or phase >= length(v):
+                    continue
                 reached, onward = phases(v)[phase]
 
                 @pl.when(reached)
@@ -194,7 +195,7 @@
         remote(piece, piece, ps.at[v], r2.at[v], partner).wait_recv()
 
     need = [
-        1 + max(v + LAG * (length(v) - 1) for v in range(9 * k + 9)) for k in range(7)
+        1 + max(v + LAGS[v] * (length(v) - 1) for v in range(9 * k + 9)) for k in range(7)
     ]
     relays(0, FIRST)
 

time: 91.3 us -> 90.1 us (0.987)
  Pallas kernels: 89.4 us -> 88.2 us
    pallas_call x1, Pallas kernels: 89.4 us -> 88.2 us  [body(): pl.pallas_call(kernel, out_shape=jax.ShapeDtypeStruct((4, 48, 512), bf16)...]
where the time goes in v3:
time: 90.1 us; the launch traced here: 89.9 us
  Pallas kernels  88.2 us (98%)
  local copies, waits for them, and re-layouts  1.76 us (2%)
    pallas_call x1, Pallas kernels, body(): pl.pallas_call(kernel, out_shape=jax.ShapeDtypeStruct((4, 48, 512), bf16)...  88.2 us

profile of v3, /device:TPU:1, one launch (start us, length us, event | category | flops | bytes accessed | tf_op | source)
XLA Modules:
  0.0 89.9 jit_solution(955746818672405908)
XLA Ops:
  0.0 88.2 %shard_map.91 = bf16[4,48,512]{2,1,0:T(8,128)(2,1)} custom-call(bf16[16,128]{1,0:T(8,128)(2,1)} %bitcast.5, bf16[9,4,384]{2,1,0:T(4,128)(2,1)} %win_in.1, f32[1,96]{1,0:T(1,128)} %bitcast.6, f32[3,2,96]{2,1,0:T(2,128)} %gain_in.1, f32[3,2,96]{2,1,0:T(2,128)} %shift_in.1, bf16[3,2,9,96,384]{4,3,2,1,0:T(8,128)(2,1)} %wres_in.1, f32[3,2,96]{2,1,0:T(2,128)} %rbias_in.1, ...), custom_call_target="tpu_custom_call" | custom-call | tf_op jit(solution)/shard_map/pallas_call | solution.py:428
  88.2 1.8 %copy.10 = bf16[48,4,512]{2,1,0:T(4,128)(2,1)} copy(bf16[48,4,512]{2,0,1:T(8,128)(2,1)} %bitcast.4) | data formatting | bytes 393216 | tf_op jit(solution)/shard_map/transpose | solution.py:480
